TPU v7x, 256 devices: a whole 4x4x8 slice. The times are simulated.
256 devices in a mesh: sec: 2 (over core), row: 4 (over x), col: 32 (over z, y).
Axes of the slice: x: 4, y: 4, z: 8, core: 2. Of those that a mesh axis runs over, the one named last changes fastest.
Arguments:
- leaf_rhs: bfloat16 [2, 4, 1, 32, 128, 256], P('sec', 'row', None, 'col'), may hold values from -6 to 6
- sep_rhs: bfloat16 [2, 4, 32, 128, 256], P('sec', 'row', 'col'), may hold values from -6 to 6
- top_rhs: bfloat16 [4, 32, 128, 256], P('row', 'col'), may hold values from -6 to 6
- leaf_inv: float32 [2, 4, 1, 32, 128, 128], P('sec', 'row', None, 'col'), may hold values from -1 to 3, as said below
- sep_inv: float32 [2, 4, 32, 128, 128], P('sec', 'row', 'col'), may hold values from -1 to 3, as said below
- top_inv: float32 [4, 32, 128, 128], P('row', 'col'), may hold values from -1 to 3, as said below
- sep_leaf: bfloat16 [2, 4, 32, 128, 4, 1, 32, 128], P('sec', 'row', None, None, None, None, 'col'), may hold values from -0.0625 to 0.0625
- top_leaf: bfloat16 [2, 4, 32, 128, 4, 1, 32, 128], P('sec', 'row', None, None, None, None, 'col'), may hold values from -0.046875 to 0.046875
- top_sep: bfloat16 [2, 4, 32, 128, 4, 32, 128], P('sec', 'row', None, None, None, 'col'), may hold values from -0.046875 to 0.046875
- sep_leaf_mask: int32 [2, 4, 32, 4, 1, 32], P('sec', 'row', None, None, None, 'col'), may hold values 0 or 1
- top_leaf_mask: int32 [2, 4, 32, 4, 1, 32], P('sec', 'row', None, None, None, 'col'), may hold values 0 or 1
- top_sep_mask: int32 [2, 4, 32, 4, 32], P('sec', 'row', None, None, 'col'), may hold values 0 or 1
Outputs:
- leaf_x: float32 [2, 4, 1, 32, 128, 256], P('sec', 'row', None, 'col')
- sep_x: float32 [2, 4, 32, 128, 256], P('sec', 'row', 'col')
- top_x: float32 [4, 32, 128, 256], P('row', 'col')
Inputs may be any that keep to these rules, and one draw needn't show every extreme that they name: `leaf_inv`: every 128 x 128 block is lower triangular with positive diagonal. `sep_inv`: every 128 x 128 block is lower triangular with positive diagonal. `top_inv`: every 128 x 128 block is lower triangular with positive diagonal.
All inputs are finite; a program needn't handle non-finite values. No bound on the sum of `sep_leaf_mask` or of `top_leaf_mask` or of `top_sep_mask` on one device may be relied on, other than what follows from the above.
Results may differ from a plain program's by a relative error of at most 0.0036.
Values may be sent and summed in bfloat16 or wider, within the bound.
A program may use at most 128 MiB of HBM per device.

v0:
```python
import jax
import jax.numpy as jnp
from jax import lax
from jax.sharding import PartitionSpec as P


def lower_apply(inverse, right_side):
    return jnp.einsum("...ab,...bn->...an", inverse, right_side, precision=lax.Precision.HIGHEST)


def upper_apply(inverse, right_side):
    return jnp.einsum("...ba,...bn->...an", inverse, right_side, precision=lax.Precision.HIGHEST)


def mask_tiles(tile_set, pattern):
    return tile_set * pattern.astype(jnp.bfloat16)[:, None, :, :, None]


def spread_down(values, update, totals):
    return update(totals, lax.all_gather(values, "row", axis=0, tiled=True), jnp.int32(0))


def reduce_row(partial_value, rhs_cols):
    col_count = lax.axis_size("col")
    summed = lax.psum_scatter(
        partial_value.reshape(col_count, partial_value.shape[0] // col_count, rhs_cols),
        "col",
        scatter_dimension=0,
        tiled=True,
    )
    return summed.reshape(summed.shape[1], rhs_cols)


def add_sections(partial_value):
    return lax.psum(partial_value, "sec")


def spread_across(values):
    return lax.all_gather(values[None], "col", axis=0, tiled=True)


def collect_up(term_fn, row_span):
    return lax.psum_scatter(
        term_fn(jnp.int32(0), row_span * lax.axis_size("row")),
        "row",
        scatter_dimension=0,
        tiled=True,
    )


def body(
    leaf_rhs,
    sep_rhs,
    top_rhs,
    leaf_inv,
    sep_inv,
    top_inv,
    sep_leaf,
    top_leaf,
    top_sep,
    sep_leaf_mask,
    top_leaf_mask,
    top_sep_mask,
):
    leaf_count = leaf_rhs.shape[2]
    tile_width = leaf_rhs.shape[4]
    rhs_cols = leaf_rhs.shape[5]
    col_count = sep_leaf.shape[2]
    row_count = sep_leaf.shape[4]
    rows_out = col_count * tile_width
    leaf_span = leaf_count * tile_width
    contract = (((0,), (0,)), ((), ()))
    sep_tiles = mask_tiles(sep_leaf[0, 0, :, :, :, :, 0], sep_leaf_mask[0, 0, :, :, :, 0])
    top_tiles = mask_tiles(top_leaf[0, 0, :, :, :, :, 0], top_leaf_mask[0, 0, :, :, :, 0])
    cross_tiles = (
        top_sep[0, 0, :, :, :, 0]
        * top_sep_mask[0, 0, :, :, 0].astype(jnp.bfloat16)[:, None, :, None]
    )
    leaf_y = lower_apply(leaf_inv[0, 0, :, 0], leaf_rhs[0, 0, :, 0].astype(jnp.float32))
    leaf_send = leaf_y.astype(jnp.bfloat16)

    def leaf_update(totals, pieces, offset):
        how_many = pieces.shape[0]
        flat_values = pieces.reshape(how_many * leaf_span, rhs_cols)
        sep_block = sep_tiles.reshape(rows_out, how_many * leaf_span)
        top_block = top_tiles.reshape(rows_out, how_many * leaf_span)
        return (
            jnp.dot(sep_block, flat_values, preferred_element_type=jnp.float32),
            jnp.dot(top_block, flat_values, preferred_element_type=jnp.float32),
        )

    empty_sum = jnp.zeros((rows_out, rhs_cols), jnp.float32)
    sep_part, top_part = spread_down(leaf_send[None], leaf_update, (empty_sum, empty_sum))
    sep_total = reduce_row(sep_part, rhs_cols)
    sep_y = lower_apply(sep_inv[0, 0, 0], sep_rhs[0, 0, 0].astype(jnp.float32) - sep_total)
    sep_send = sep_y.astype(jnp.bfloat16)

    def sep_update(totals, pieces, offset):
        how_many = pieces.shape[0]
        tile_block = cross_tiles.reshape(rows_out, how_many * tile_width)
        return totals + jnp.dot(
            tile_block,
            pieces.reshape(how_many * tile_width, rhs_cols),
            preferred_element_type=jnp.float32,
        )

    top_part = spread_down(sep_send[None], sep_update, top_part)
    top_total = reduce_row(add_sections(top_part), rhs_cols)
    top_y = lower_apply(top_inv[0, 0], top_rhs[0, 0].astype(jnp.float32) - top_total)
    top_x = upper_apply(top_inv[0, 0], top_y)
    top_flat = spread_across(top_x.astype(jnp.bfloat16)).reshape(rows_out, rhs_cols)
    cross_flat = cross_tiles.reshape(rows_out, row_count * tile_width)
    sep_flat_tiles = sep_tiles.reshape(rows_out, row_count * leaf_span)
    top_flat_tiles = top_tiles.reshape(rows_out, row_count * leaf_span)

    def sep_terms(offset, how_many):
        return lax.dot_general(cross_flat, top_flat, contract, preferred_element_type=jnp.float32)

    sep_t = collect_up(sep_terms, tile_width)
    sep_x = upper_apply(sep_inv[0, 0, 0], sep_y - sep_t)
    sep_row = spread_across(sep_x.astype(jnp.bfloat16)).reshape(rows_out, rhs_cols)

    def both_terms(offset, how_many):
        return lax.dot_general(
            sep_flat_tiles, sep_row, contract, preferred_element_type=jnp.float32
        ) + lax.dot_general(top_flat_tiles, top_flat, contract, preferred_element_type=jnp.float32)

    leaf_t = collect_up(both_terms, leaf_span)
    leaf_x = upper_apply(
        leaf_inv[0, 0, :, 0], leaf_y - leaf_t.reshape(leaf_count, tile_width, rhs_cols)
    )
    return (leaf_x[None, None, :, None], sep_x[None, None, None], top_x[None, None])


def solution(mesh):
    in_specs = (
        P("sec", "row", None, "col", None, None),
        P("sec", "row", "col", None, None),
        P("row", "col", None, None),
        P("sec", "row", None, "col", None, None),
        P("sec", "row", "col", None, None),
        P("row", "col", None, None),
        P("sec", "row", None, None, None, None, "col", None),
        P("sec", "row", None, None, None, None, "col", None),
        P("sec", "row", None, None, None, "col", None),
        P("sec", "row", None, None, None, "col"),
        P("sec", "row", None, None, None, "col"),
        P("sec", "row", None, None, "col"),
    )
    out_specs = (
        P("sec", "row", None, "col", None, None),
        P("sec", "row", "col", None, None),
        P("row", "col", None, None),
    )
    return jax.shard_map(body, mesh=mesh, in_specs=in_specs, out_specs=out_specs, check_vma=False)
```

profile of v0, /device:TPU:8, one launch (start us, length us, event | category | flops | bytes accessed | tf_op | source)
XLA Modules:
  0.0 758.6 jit_solution(15964059549455217081)
XLA Ops:
  7.2 1.1 fusion.38
  8.3 12.6 %all-gather = bf16[512,256]{1,0:T(8,128)(2,1)S(1)} all-gather(bf16[128,256]{1,0:T(8,128)(2,1)S(1)} %get-tuple-element.6), channel_id=2, replica_groups=mesh['sec'=2,'row'=4,'col'=32] {'row'}, dimensions={0}, use_global_device_ids=true | all-gather | bytes 327680 | tf_op jit(solution)/shard_map/all_gather | solution.py:20
  20.9 0.7 convert_element_type.74
  21.7 6.0 broadcast_multiply_fusion.2
  27.7 7.2 mul.49
  34.9 5.4 fusion.17
  40.4 0.6 copy-done.7
  41.2 4.0 broadcast_multiply_fusion
  45.3 3.3 fusion.5
  48.5 0.8 copy-done.1
  49.4 1.0 copy-done.2
  50.4 3.8 broadcast_multiply_fusion.1
  54.2 211.2 %reduce-scatter.5.cloned.1.call-done = f32[1,128,256]{2,1,0:T(8,128)} async-done(((f32[32,128,256]{2,1,0:T(8,128)}), f32[1,128,256]{2,1,0:T(8,128)}) %reduce-scatter.5.cloned.1.call-update) | async-done | bytes 131088 | tf_op jit(solution)/shard_map/reduce_scatter | solution.py:25
  265.4 1.3 fusion.39
  266.7 11.9 %all-gather.1 = bf16[512,256]{0,1:T(8,128)(2,1)S(1)} all-gather(bf16[128,256]{0,1:T(8,128)(2,1)S(1)} %get-tuple-element.8), channel_id=3, replica_groups=mesh['sec'=2,'row'=4,'col'=32] {'row'}, dimensions={0}, use_global_device_ids=true | all-gather | bytes 327680 | tf_op jit(solution)/shard_map/all_gather | solution.py:20
  278.6 6.7 convolution_add_fusion
  285.4 220.9 %reduce-scatter.11.cloned.1.call-done = f32[1,128,256]{2,1,0:T(8,128)} async-done(((f32[32,128,256]{2,1,0:T(8,128)}), f32[1,128,256]{2,1,0:T(8,128)}) %reduce-scatter.11.cloned.1.call-update) | async-done | bytes 131088 | tf_op jit(solution)/shard_map/reduce_scatter | solution.py:25
  506.3 30.3 %all-reduce.2.cloned.1.call-done = f32[1,128,256]{2,1,0:T(8,128)} async-done(((f32[1,128,256]{2,1,0:T(8,128)}), f32[1,128,256]{2,1,0:T(8,128)}) %all-reduce.2.cloned.1.call-update) | async-done | bytes 131088 | tf_op jit(solution)/shard_map/psum | solution.py:35
  536.6 1.3 fusion.20
  537.9 0.9 bitcast_convert_fusion.1
  539.1 76.2 %all-gather.7.cloned.1.call-done = bf16[4096,256]{0,1:T(8,128)(2,1)} async-done(((bf16[128,256]{0,1:T(8,128)(2,1)}), bf16[4096,256]{0,1:T(8,128)(2,1)}) %all-gather.7.cloned.1.call-update) | async-done | bytes 2097168 | tf_op jit(solution)/shard_map/all_gather | solution.py:39
  615.2 5.0 fusion
  620.3 23.6 %reduce-scatter.7.cloned.1.call-done = f32[128,256]{0,1:T(8,128)} async-done(((f32[512,256]{0,1:T(8,128)}), f32[128,256]{0,1:T(8,128)}) %reduce-scatter.7.cloned.1.call-update) | async-done | bytes 131088 | tf_op jit(solution)/shard_map/reduce_scatter | solution.py:43
  643.9 1.8 bitcast_convert_fusion
  645.8 3.5 fusion.3
  649.3 71.8 %all-gather.9.cloned.1.call-done = bf16[4096,256]{0,1:T(8,128)(2,1)} async-done(((bf16[128,256]{0,1:T(8,128)(2,1)}), bf16[4096,256]{0,1:T(8,128)(2,1)}) %all-gather.9.cloned.1.call-update) | async-done | bytes 2097168 | tf_op jit(solution)/shard_map/all_gather | solution.py:39
  721.0 5.0 fusion.14
  726.1 0.8 copy.20
  726.8 0.8 copy.19
  727.6 22.1 %reduce-scatter.9.cloned.1.call-done = f32[128,256]{1,0:T(8,128)} async-done(((f32[512,256]{1,0:T(8,128)}), f32[128,256]{1,0:T(8,128)}) %reduce-scatter.9.cloned.1.call-update) | async-done | bytes 131088 | tf_op jit(solution)/shard_map/reduce_scatter | solution.py:43
  749.7 1.3 convolution_bitcast_fusion
  751.0 0.8 copy.18
  (36 shorter events, 0.9 us)
Async XLA Ops:
  7.2 258.3 %copy-start = (f32[1,1,1,128,128]{4,3,2,1,0:T(8,128)S(1)}, f32[1,1,1,128,128]{4,3,2,1,0:T(8,128)}, u32[]{:S(2)}) copy-start(f32[1,1,1,128,128]{4,3,2,1,0:T(8,128)} %param.16) | copy-start | bytes 196612
  7.2 258.2 %reduce-scatter.5.cloned.1.call-start = ((), (), s32[]{:S(2)}) async-start(), calls=%async_computation.4 | async-start | bytes 4325376 | tf_op jit(solution)/shard_map/reduce_scatter | solution.py:25
  40.3 0.7 copy-start.7
  40.3 0.8 copy-start.8
  40.3 465.9 %reduce-scatter.11.cloned.1.call-start = ((), (), s32[]{:S(2)}) async-start(), calls=%async_computation.9 | async-start | bytes 4325376 | tf_op jit(solution)/shard_map/reduce_scatter | solution.py:25
  45.2 4.1 copy-start.1
  45.3 5.1 copy-start.2
  50.4 215.1 %copy-start.5 = (bf16[1,1,1,128,256]{4,3,2,1,0:T(8,128)(2,1)S(1)}, bf16[1,1,1,128,256]{4,3,2,1,0:T(8,128)(2,1)}, u32[]{:S(2)}) copy-start(bf16[1,1,1,128,256]{4,3,2,1,0:T(8,128)(2,1)} %param.13) | copy-start | bytes 196612
  285.3 251.3 %copy-start.4 = (f32[1,1,128,128]{3,2,1,0:T(8,128)S(1)}, f32[1,1,128,128]{3,2,1,0:T(8,128)}, u32[]{:S(2)}) copy-start(f32[1,1,128,128]{3,2,1,0:T(8,128)} %param.17) | copy-start | bytes 196612
  285.3 251.3 %copy-start.6 = (bf16[1,1,128,256]{3,2,1,0:T(8,128)(2,1)S(1)}, bf16[1,1,128,256]{3,2,1,0:T(8,128)(2,1)}, u32[]{:S(2)}) copy-start(bf16[1,1,128,256]{3,2,1,0:T(8,128)(2,1)} %param.14) | copy-start | bytes 196612
  285.3 251.3 %all-reduce.2.cloned.1.call-start = ((), (), s32[]{:S(2)}) async-start(), calls=%async_computation.10 | async-start | bytes 262144 | tf_op jit(solution)/shard_map/psum | solution.py:35
  506.3 109.0 %all-gather.7.cloned.1.call-start = ((), (), s32[]{:S(2)}) async-start(), calls=%async_computation.7 | async-start | bytes 2162688 | tf_op jit(solution)/shard_map/all_gather | solution.py:39
  538.8 105.1 %reduce-scatter.7.cloned.1.call-start = ((), (), s32[]{:S(2)}) async-start(), calls=%async_computation.5 | async-start | bytes 655360 | tf_op jit(solution)/shard_map/reduce_scatter | solution.py:43
  615.2 30.5 %copy-start.9 = (bf16[4096,256]{0,1:T(8,128)(2,1)S(1)}, bf16[4096,256]{0,1:T(8,128)(2,1)}, u32[]{:S(2)}) copy-start(bf16[4096,256]{0,1:T(8,128)(2,1)} %all-gather.7.cloned.1.call-done) | copy-start | bytes 6291460
  620.3 100.8 %all-gather.9.cloned.1.call-start = ((), (), s32[]{:S(2)}) async-start(), calls=%async_computation.8 | async-start | bytes 2162688 | tf_op jit(solution)/shard_map/all_gather | solution.py:39
  645.7 104.0 %reduce-scatter.9.cloned.1.call-start = ((), (), s32[]{:S(2)}) async-start(), calls=%async_computation.6 | async-start | bytes 655360 | tf_op jit(solution)/shard_map/reduce_scatter | solution.py:43
  721.0 28.7 %copy-start.3 = (f32[1,1,1,1,128,128]{5,4,3,2,1,0:T(8,128)S(1)}, f32[1,1,1,1,128,128]{5,4,3,2,1,0:T(8,128)}, u32[]{:S(2)}) copy-start(f32[1,1,1,1,128,128]{5,4,3,2,1,0:T(8,128)} %param.15) | copy-start | bytes 196612
Sparse Core Ops, SparseCore 0:
  40.4 224.9 reduce-scatter.4
  285.4 220.7 reduce-scatter.10
  508.8 27.7 all-reduce.1
  539.5 75.6 all-gather.6
  620.4 23.4 reduce-scatter.6
  646.8 74.1 all-gather.8
  726.2 23.4 reduce-scatter.8
where the time goes:
time: 759 us
  waiting for transfers between devices  656 us (86%)
  matrix products  36.5 us (5%)
  blocking collectives  24.5 us (3%)
  other arithmetic  14.6 us (2%)
  between operations  14.2 us (2%)
  local copies, waits for them, and re-layouts  12.3 us (2%)
    reduce_scatter x2, waiting for transfers between devices, reduce_row(): lax.psum_scatter(partial_value.reshape(col_count, partial_value.shape[0]...  432 us
    all_gather x2, waiting for transfers between devices, spread_across(): return lax.all_gather(values[None], 'col', axis=0, tiled=True)  148 us
    reduce_scatter x2, waiting for transfers between devices, collect_up(): lax.psum_scatter(term_fn(jnp.int32(0), row_span * lax.axis_size('row')),...  45.7 us
    psum x1, waiting for transfers between devices, add_sections(): return lax.psum(partial_value, 'sec')  30.3 us
    all_gather x2, blocking collectives, spread_down(): lax.all_gather(values, 'row', axis=0, tiled=True)  24.5 us
  transfers between devices with their start and end apart: 7, of which 7 were waited for; matrix products, arithmetic and copies ran while one was open for 2% of the time, Pallas kernels for 0%

commit v1 on v0

--- a/solution.py
+++ b/solution.py
@@ -2,6 +2,13 @@
 import jax.numpy as jnp
 from jax import lax
 from jax.sharding import PartitionSpec as P
+
+
+def windows_store(inputs):
+    t1 = jnp.concatenate(
+        jax.lax.all_to_all(jnp.stack([inputs] * jax.lax.axis_size("col"), 0), "col", 0, 0), 0
+    )
+    return t1
 
 
 def lower_apply(inverse, right_side):
@@ -36,7 +43,7 @@
 
 
 def spread_across(values):
-    return lax.all_gather(values[None], "col", axis=0, tiled=True)
+    return windows_store(values[None])
 
 
 def collect_up(term_fn, row_span):

time: 759 us -> 718 us (0.946)
  waiting for transfers between devices: 656 us -> 546 us
  blocking collectives: 24.5 us -> 85.7 us
  starting transfers between devices: 0.47 us -> 10.4 us
    all_gather x2 -> x0, waiting for transfers between devices: 148 us -> none  [spread_across(): return lax.all_gather(values[None], 'col', axis=0, tiled=True)]
    all_to_all x0 -> x1, blocking collectives: none -> 61.2 us  [windows_store(): jax.lax.all_to_all(jnp.stack([inputs] * jax.lax.axis_size('col'), 0), 'co...]
    all_to_all x0 -> x1, waiting for transfers between devices: none -> 44 us  [windows_store(): jax.lax.all_to_all(jnp.stack([inputs] * jax.lax.axis_size('col'), 0), 'co...]
    all_to_all x0 -> x1, starting transfers between devices: none -> 10.2 us  [windows_store(): jax.lax.all_to_all(jnp.stack([inputs] * jax.lax.axis_size('col'), 0), 'co...]
  transfers between devices with their start and end apart: 7 -> 6, of which waited for: 7 -> 6; matrix products, arithmetic and copies ran while one was open for 2% -> 2% of each run, Pallas kernels for 0% -> 0%
where the time goes in v1:
time: 718 us
  waiting for transfers between devices  546 us (76%)
  blocking collectives  85.7 us (12%)
  matrix products  32.3 us (4%)
  other arithmetic  14.6 us (2%)
  local copies, waits for them, and re-layouts  14.3 us (2%)
  between operations  13.9 us (2%)
  starting transfers between devices  10.4 us (1%)
    reduce_scatter x2, waiting for transfers between devices, reduce_row(): lax.psum_scatter(partial_value.reshape(col_count, partial_value.shape[0]...  432 us
    all_to_all x1, blocking collectives, windows_store(): jax.lax.all_to_all(jnp.stack([inputs] * jax.lax.axis_size('col'), 0), 'co...  61.2 us
    all_to_all x1, waiting for transfers between devices, windows_store(): jax.lax.all_to_all(jnp.stack([inputs] * jax.lax.axis_size('col'), 0), 'co...  44 us
    reduce_scatter x2, waiting for transfers between devices, collect_up(): lax.psum_scatter(term_fn(jnp.int32(0), row_span * lax.axis_size('row')),...  39.7 us
    psum x1, waiting for transfers between devices, add_sections(): return lax.psum(partial_value, 'sec')  30.4 us
    all_gather x2, blocking collectives, spread_down(): lax.all_gather(values, 'row', axis=0, tiled=True)  24.5 us
  transfers between devices with their start and end apart: 6, of which 6 were waited for; matrix products, arithmetic and copies ran while one was open for 2% of the time, Pallas kernels for 0%

profile of v1, /device:TPU:8, one launch (start us, length us, event | category | flops | bytes accessed | tf_op | source)
XLA Modules:
  0.0 717.5 jit_solution(5074801009649368815)
XLA Ops:
  7.2 1.1 fusion.38
  8.3 12.6 %all-gather = bf16[512,256]{1,0:T(8,128)(2,1)S(1)} all-gather(bf16[128,256]{1,0:T(8,128)(2,1)S(1)} %get-tuple-element.6), channel_id=2, replica_groups=mesh['sec'=2,'row'=4,'col'=32] {'row'}, dimensions={0}, use_global_device_ids=true | all-gather | bytes 327680 | tf_op jit(solution)/shard_map/all_gather | solution.py:27
  20.9 0.7 convert_element_type.74
  21.7 6.0 broadcast_multiply_fusion.2
  27.7 7.3 %mul.49 = bf16[32,128,512]{2,1,0:T(8,128)(2,1)} reshape(bf16[1,1,32,128,4,1,1,128]{7,4,6,5,3,2,1,0:T(4,128)(2,1)} %broadcast_multiply_fusion.2) | data formatting | bytes 8388608 | tf_op jit(solution)/shard_map/mul | solution.py:23
  35.0 5.4 fusion.17
  41.3 4.0 broadcast_multiply_fusion
  45.3 3.3 fusion.2
  48.6 0.8 copy-done.2
  49.4 1.0 copy-done.3
  50.4 3.8 broadcast_multiply_fusion.1
  54.2 211.3 %reduce-scatter.5.cloned.1.call-done = f32[1,128,256]{2,1,0:T(8,128)} async-done(((f32[32,128,256]{2,1,0:T(8,128)}), f32[1,128,256]{2,1,0:T(8,128)}) %reduce-scatter.5.cloned.1.call-update) | async-done | bytes 131088 | tf_op jit(solution)/shard_map/reduce_scatter | solution.py:32
  265.5 1.3 fusion.39
  266.8 11.9 %all-gather.1 = bf16[512,256]{0,1:T(8,128)(2,1)S(1)} all-gather(bf16[128,256]{0,1:T(8,128)(2,1)S(1)} %get-tuple-element.8), channel_id=3, replica_groups=mesh['sec'=2,'row'=4,'col'=32] {'row'}, dimensions={0}, use_global_device_ids=true | all-gather | bytes 327680 | tf_op jit(solution)/shard_map/all_gather | solution.py:27
  278.7 6.7 convolution_add_fusion
  285.5 220.9 %reduce-scatter.11.cloned.1.call-done = f32[1,128,256]{2,1,0:T(8,128)} async-done(((f32[32,128,256]{2,1,0:T(8,128)}), f32[1,128,256]{2,1,0:T(8,128)}) %reduce-scatter.11.cloned.1.call-update) | async-done | bytes 131088 | tf_op jit(solution)/shard_map/reduce_scatter | solution.py:32
  506.5 30.4 %all-reduce.2.cloned.1.call-done = f32[1,128,256]{2,1,0:T(8,128)} async-done(((f32[1,128,256]{2,1,0:T(8,128)}), f32[1,128,256]{2,1,0:T(8,128)}) %all-reduce.2.cloned.1.call-update) | async-done | bytes 131088 | tf_op jit(solution)/shard_map/psum | solution.py:42
  536.8 1.3 fusion.20
  538.8 61.2 %all_to_all.10 = bf16[32,1,128,256]{3,2,1,0:T(8,128)(2,1)S(1)} all-to-all(bf16[32,1,128,256]{3,2,1,0:T(8,128)(2,1)S(1)} %stack.6), channel_id=1, replica_groups=mesh['sec'=2,'row'=4,'col'=32] {'col'}, dimensions={0} | all-to-all | bytes 4194304 | tf_op jit(solution)/shard_map/all_to_all | solution.py:9
  599.9 2.1 fusion.4
  602.1 21.0 %reduce-scatter.7.cloned.1.call-done = f32[128,256]{0,1:T(8,128)} async-done(((f32[512,256]{0,1:T(8,128)}), f32[128,256]{0,1:T(8,128)}) %reduce-scatter.7.cloned.1.call-update) | async-done | bytes 131088 | tf_op jit(solution)/shard_map/reduce_scatter | solution.py:50
  623.1 1.2 bitcast_convert_fusion
  624.4 1.6 stack.7
  626.0 10.2 %all-to-all-start.1 = ((bf16[32,1,128,256]{3,2,1,0:T(8,128)(2,1)}), bf16[32,1,128,256]{3,2,1,0:T(8,128)(2,1)}, u32[]{:S(2)}, u32[]{:S(2)}) async-start(bf16[32,1,128,256]{3,2,1,0:T(8,128)(2,1)} %stack.7), calls=%async_computation.3 | async-start | bytes 4194304 | tf_op jit(solution)/shard_map/all_to_all | solution.py:9
  636.3 3.5 fusion
  639.8 44.0 %all-to-all-done.1 = bf16[32,1,128,256]{3,2,1,0:T(8,128)(2,1)} async-done(((bf16[32,1,128,256]{3,2,1,0:T(8,128)(2,1)}), bf16[32,1,128,256]{3,2,1,0:T(8,128)(2,1)}, u32[]{:S(2)}, u32[]{:S(2)}) %all-to-all-start.1) | async-done | bytes 2097184 | tf_op jit(solution)/shard_map/all_to_all | solution.py:9
  683.7 5.0 fusion.14
  688.7 0.8 copy.22
  689.5 0.8 copy.21
  690.3 18.7 %reduce-scatter.9.cloned.1.call-done = f32[128,256]{1,0:T(8,128)} async-done(((f32[512,256]{1,0:T(8,128)}), f32[128,256]{1,0:T(8,128)}) %reduce-scatter.9.cloned.1.call-update) | async-done | bytes 131088 | tf_op jit(solution)/shard_map/reduce_scatter | solution.py:50
  709.0 1.3 convolution_bitcast_fusion
  710.3 0.8 copy.20
  (37 shorter events, 1.9 us)
Async XLA Ops:
  7.2 258.3 %copy-start = (f32[1,1,1,128,128]{4,3,2,1,0:T(8,128)S(1)}, f32[1,1,1,128,128]{4,3,2,1,0:T(8,128)}, u32[]{:S(2)}) copy-start(f32[1,1,1,128,128]{4,3,2,1,0:T(8,128)} %param.16) | copy-start | bytes 196612
  7.2 258.3 %reduce-scatter.5.cloned.1.call-start = ((), (), s32[]{:S(2)}) async-start(), calls=%async_computation.6 | async-start | bytes 4325376 | tf_op jit(solution)/shard_map/reduce_scatter | solution.py:32
  40.4 0.7 copy-start.8
  40.4 0.8 copy-start.9
  40.4 466.0 %reduce-scatter.11.cloned.1.call-start = ((), (), s32[]{:S(2)}) async-start(), calls=%async_computation.9 | async-start | bytes 4325376 | tf_op jit(solution)/shard_map/reduce_scatter | solution.py:32
  45.3 4.1 copy-start.2
  45.3 5.1 copy-start.3
  50.4 215.1 %copy-start.6 = (bf16[1,1,1,128,256]{4,3,2,1,0:T(8,128)(2,1)S(1)}, bf16[1,1,1,128,256]{4,3,2,1,0:T(8,128)(2,1)}, u32[]{:S(2)}) copy-start(bf16[1,1,1,128,256]{4,3,2,1,0:T(8,128)(2,1)} %param.13) | copy-start | bytes 196612
  285.4 251.4 %copy-start.5 = (f32[1,1,128,128]{3,2,1,0:T(8,128)S(1)}, f32[1,1,128,128]{3,2,1,0:T(8,128)}, u32[]{:S(2)}) copy-start(f32[1,1,128,128]{3,2,1,0:T(8,128)} %param.17) | copy-start | bytes 196612
  285.4 251.4 %copy-start.7 = (bf16[1,1,128,256]{3,2,1,0:T(8,128)(2,1)S(1)}, bf16[1,1,128,256]{3,2,1,0:T(8,128)(2,1)}, u32[]{:S(2)}) copy-start(bf16[1,1,128,256]{3,2,1,0:T(8,128)(2,1)} %param.14) | copy-start | bytes 196612
  285.4 251.4 %all-reduce.2.cloned.1.call-start = ((), (), s32[]{:S(2)}) async-start(), calls=%async_computation.10 | async-start | bytes 262144 | tf_op jit(solution)/shard_map/psum | solution.py:42
  506.4 116.7 %reduce-scatter.7.cloned.1.call-start = ((), (), s32[]{:S(2)}) async-start(), calls=%async_computation.7 | async-start | bytes 655360 | tf_op jit(solution)/shard_map/reduce_scatter | solution.py:50
  538.5 61.4 %copy-start.1 = (bf16[1,1,32,128,4,1,128]{6,4,5,3,2,1,0:T(4,128)(2,1)S(1)}, bf16[1,1,32,128,4,1,128]{6,4,5,3,2,1,0:T(4,128)(2,1)}, u32[]{:S(2)}) copy-start(bf16[1,1,32,128,4,1,128]{6,4,5,3,2,1,0:T(4,128)(2,1)} %broadcast_multiply_fusion.1) | copy-start | bytes 12582916
  626.0 57.8 %all-to-all-start.1 = ((bf16[32,1,128,256]{3,2,1,0:T(8,128)(2,1)}), bf16[32,1,128,256]{3,2,1,0:T(8,128)(2,1)}, u32[]{:S(2)}, u32[]{:S(2)}) async-start(bf16[32,1,128,256]{3,2,1,0:T(8,128)(2,1)} %stack.7), calls=%async_computation.3 | async-start | bytes 4194304 | tf_op jit(solution)/shard_map/all_to_all | solution.py:9
  636.2 72.7 %reduce-scatter.9.cloned.1.call-start = ((), (), s32[]{:S(2)}) async-start(), calls=%async_computation.8 | async-start | bytes 655360 | tf_op jit(solution)/shard_map/reduce_scatter | solution.py:50
  683.7 25.2 %copy-start.4 = (f32[1,1,1,1,128,128]{5,4,3,2,1,0:T(8,128)S(1)}, f32[1,1,1,1,128,128]{5,4,3,2,1,0:T(8,128)}, u32[]{:S(2)}) copy-start(f32[1,1,1,1,128,128]{5,4,3,2,1,0:T(8,128)} %param.15) | copy-start | bytes 196612
Sparse Core Ops, SparseCore 0:
  40.5 224.9 reduce-scatter.4
  285.5 220.7 reduce-scatter.10
  508.9 27.8 all-reduce.1
  602.2 20.8 reduce-scatter.6
  688.9 20.0 reduce-scatter.8
